TPU v7x, 256 devices: a whole 4x4x8 slice. The times are simulated.
256 devices in a mesh: stripe: 32 (over z, x_lo, core), tile: 8 (over y, x_hi).
Axes of the slice: x: 4 (x_hi: 2, x_lo: 2; x = x_hi * 2 + x_lo), y: 4, z: 8, core: 2. Of those that a mesh axis runs over, the one named last changes fastest.
Arguments:
- positions: int32 [32, 24], P('stripe', 'tile'), may hold values from -64 to -64, as said below
- row_offsets: int32 [32, 24], P('stripe', 'tile'), may hold values from -64 to 64, as said below
- amplitudes: float32 [32, 24, 256, 256], P('stripe', 'tile'), may hold values from 0 to 2
- object_field: float32 [2, 8192, 1024], P(None, 'stripe', 'tile'), may hold values from -6 to 6
- probe_field: float32 [2, 256, 256], replicated, may hold values from -6 to 6
Outputs:
- object_out: float32 [2, 8192, 1024], P(None, 'stripe', 'tile')
- probe_out: float32 [2, 256, 256], replicated
Inputs may be any that keep to these rules, and one draw needn't show every extreme that they name: `positions`: in every block of 3 patterns of one stripe and one tile, the first offset is -64 and the second is 128 - 192. `row_offsets`: in every block of 3 patterns of one stripe and one tile, the first row offset is -64 and the second is 64.
All inputs are finite; a program needn't handle non-finite values.
Results may differ from a plain program's by a relative error of at most 0.0006.
The roundings to bfloat16 on the way count: a program that leaves them out, or rounds other values in their place, can miss the bound.
Values sent between devices are 32-bit elements; how exact they have to be, the bound alone decides.
No kernel may reach another device: no remote copies, remote signals or barrier semaphores. Data moves between devices by JAX's collectives and lax.ppermute only.
A program may use at most 64 MiB of HBM per device.

v0:
```python
import math
import jax
import jax.numpy as jnp
from jax import lax
from jax.sharding import PartitionSpec as P

PW = 256
HALO = 64
TILE_W = 128
PAT_DEV = 3
INNER = 2
OUTER = 2


def padded(x, sides, width):
    for axis, dim in sides:
        count, length = (lax.axis_size(axis), x.shape[dim])
        up = [(i, (i + 1) % count) for i in range(count - 1)]
        down = [(j, i) for i, j in up]
        last = lax.slice_in_dim(x, length - width, length, axis=dim)
        first = lax.slice_in_dim(x, 0, width, axis=dim)
        before = lax.ppermute(last, axis, up)
        after = lax.ppermute(first, axis, down)
        x = jnp.concatenate([before, x, after], axis=dim)
    return x


def from_behind(value, axis, steps):
    count = lax.axis_size(axis)
    first, last = (max(0, -steps), min(count, count - steps))
    return lax.ppermute(value, axis, [(source, source + steps) for source in range(first, last)])


def dft_tables():
    indices = jnp.arange(PW, dtype=jnp.int32)
    phase = indices[:, None] * indices[None, :] % PW
    angles = phase.astype(jnp.float32) * (2.0 * math.pi / PW)
    factor = 1.0 / math.sqrt(PW)
    return (
        (jnp.cos(angles) * factor).astype(jnp.bfloat16),
        (jnp.sin(angles) * factor).astype(jnp.bfloat16),
    )


def apply_left(matrix, batch):
    return jnp.einsum("kn,pnm->pkm", matrix, batch, preferred_element_type=jnp.float32)


def apply_right(batch, matrix):
    return jnp.einsum("pkn,nm->pkm", batch, matrix, preferred_element_type=jnp.float32)


def pattern_pass(windows, probe_field, measured, cosine, sine):
    win_re = windows[:, 0]
    win_im = windows[:, 1]
    probe_re = probe_field[0]
    probe_im = probe_field[1]
    exit_re = (probe_re * win_re - probe_im * win_im).astype(jnp.bfloat16)
    exit_im = (probe_re * win_im + probe_im * win_re).astype(jnp.bfloat16)
    half_re = (apply_left(cosine, exit_re) + apply_left(sine, exit_im)).astype(jnp.bfloat16)
    half_im = (apply_left(cosine, exit_im) - apply_left(sine, exit_re)).astype(jnp.bfloat16)
    spec_re = apply_right(half_re, cosine) + apply_right(half_im, sine)
    spec_im = apply_right(half_im, cosine) - apply_right(half_re, sine)
    magnitude = jnp.sqrt(spec_re * spec_re + spec_im * spec_im)
    scaling = measured / jnp.maximum(magnitude, 0.5)
    miss_re = (spec_re - scaling * spec_re).astype(jnp.bfloat16)
    miss_im = (spec_im - scaling * spec_im).astype(jnp.bfloat16)
    hb_re = (apply_left(cosine, miss_re) - apply_left(sine, miss_im)).astype(jnp.bfloat16)
    hb_im = (apply_left(cosine, miss_im) + apply_left(sine, miss_re)).astype(jnp.bfloat16)
    back_re = apply_right(hb_re, cosine) - apply_right(hb_im, sine)
    back_im = apply_right(hb_im, cosine) + apply_right(hb_re, sine)
    object_grad = jnp.stack(
        [probe_re * back_re + probe_im * back_im, probe_re * back_im - probe_im * back_re], axis=1
    )
    probe_grad = jnp.stack(
        [
            jnp.sum(win_re * back_re + win_im * back_im, axis=0),
            jnp.sum(win_re * back_im - win_im * back_re, axis=0),
        ]
    )
    illumination = jnp.sum(win_re * win_re + win_im * win_im, axis=0)
    return (object_grad, probe_grad, illumination)


def per_device(positions, row_offsets, amplitudes, object_field, probe_field):
    cosine, sine = dft_tables()
    column_starts = positions[0] + HALO
    row_starts = row_offsets[0] + HALO
    measured = amplitudes[0]
    rows_ext = PW + 2 * HALO
    columns_ext = TILE_W + 2 * HALO
    zero_index = jnp.zeros((), jnp.int32)
    current = object_field
    extended = object_field
    for outer_step in range(OUTER):
        grad_sum = jnp.zeros((2, PW, PW), jnp.float32)
        light_sum = jnp.zeros((PW, PW), jnp.float32)
        step_size = 1.0 / (
            2.0
            * PAT_DEV
            * jnp.max(probe_field[0] * probe_field[0] + probe_field[1] * probe_field[1])
            + 1e-06
        )
        for inner_step in range(INNER):
            extended = padded(current, (("stripe", 1), ("tile", 2)), HALO)
            windows = jax.vmap(
                lambda row_start, column_start: lax.dynamic_slice(
                    extended, (zero_index, row_start, column_start), (2, PW, PW)
                )
            )(row_starts, column_starts)
            object_grad, grad_sum, light_sum = pattern_pass(
                windows, probe_field, measured, cosine, sine
            )
            gradient = jnp.zeros((2, rows_ext, columns_ext), jnp.float32)
            for pattern in range(PAT_DEV):
                where = (zero_index, row_starts[pattern], column_starts[pattern])
                before = lax.dynamic_slice(gradient, where, (2, PW, PW))
                gradient = lax.dynamic_update_slice(gradient, before + object_grad[pattern], where)
            from_left = from_behind(gradient[:, :, HALO + TILE_W :], "tile", 1)
            from_right = from_behind(gradient[:, :, :HALO], "tile", -1)
            middle = gradient[:, :, HALO : HALO + TILE_W]
            middle = middle.at[:, :, :HALO].add(from_left)
            middle = middle.at[:, :, TILE_W - HALO :].add(from_right)
            from_above = from_behind(middle[:, HALO + PW :, :], "stripe", 1)
            from_below = from_behind(middle[:, :HALO, :], "stripe", -1)
            own_grad = middle[:, HALO : HALO + PW, :]
            own_grad = own_grad.at[:, :HALO, :].add(from_above)
            own_grad = own_grad.at[:, PW - HALO :, :].add(from_below)
            current = current - step_size * own_grad
        total_grad, total_light = lax.psum((grad_sum, light_sum), ("stripe", "tile"))
        probe_field = probe_field - 0.5 * total_grad / (total_light + 1.0)
    return (current, probe_field)


def solution(mesh):
    placed = (
        P("stripe", "tile"),
        P("stripe", "tile"),
        P("stripe", "tile", None, None),
        P(None, "stripe", "tile"),
        P(),
    )
    return jax.shard_map(
        per_device,
        mesh=mesh,
        in_specs=placed,
        out_specs=(P(None, "stripe", "tile"), P()),
        check_vma=False,
    )
```

profile of v0, /device:TPU:2, one launch (start us, length us, event | category | flops | bytes accessed | tf_op | source)
XLA Modules:
  0.0 924.7 jit_solution(10686164837930913628)
XLA Ops:
  21.8 4.1 collective-permute-start.2
  27.2 7.7 collective-permute-done.2
  35.0 11.0 %collective-permute-done.3 = f32[2,384,64]{2,0,1:T(2,128)S(1)} collective-permute-done((f32[2,384,64]{2,0,1:T(2,128)S(1)}, f32[2,384,64]{2,0,1:T(2,128)S(1)}, u32[]{:S(2)}, u32[]{:S(2)}) %collective-permute-start.3) | collective-permute-done | bytes 196640 | tf_op jit(solution)/shard_map/ppermute | solution.py:23
  70.4 12.6 %subtract_bitcast_fusion.3 = (f32[3,1,256,256]{3,2,0,1:T(8,128)S(1)}, f32[3,1,256,256]{3,2,0,1:T(8,128)S(1)}) fusion(f32[3,256,256]{2,1,0:T(8,128)S(1)} %convolution_add_fusion.12, f32[256,256]{1,0:T(8,128)S(1)} %get-tuple-element.251, f32[256,256]{1,0:T(8,128)S(1)} %get-tuple-element.250, f32[3,256,256]{2,1,0:T(8,128)S(1)} %fusion.160, ...), kind=kOutput, calls=%fused_computation.134 | convolution fusion | flops 103088128 | bytes 4063232 | tf_op jit(solution)/shard_map/pkn,nm->pkm/dot_general | solution.py:50
  90.8 4.5 collective-permute-start.4
  96.7 7.2 collective-permute-done.4
  105.1 9.0 collective-permute-done.5
  132.5 5.2 collective-permute-start.10
  139.0 7.8 collective-permute-done.10
  146.8 9.7 %collective-permute-done.11 = f32[2,384,64]{2,1,0:T(8,128)S(1)} collective-permute-done((f32[2,384,64]{2,1,0:T(8,128)S(1)}, f32[2,384,64]{2,1,0:T(8,128)S(1)}, u32[]{:S(2)}, u32[]{:S(2)}) %collective-permute-start.11) | collective-permute-done | bytes 196640 | tf_op jit(solution)/shard_map/ppermute | solution.py:23
  191.4 5.3 collective-permute-start.12
  198.2 8.0 collective-permute-done.12
  207.2 8.2 collective-permute-done.13
  224.7 5.0 collective-permute-start.16
  236.4 251.6 %all-reduce.7.cloned.1.call-done = (f32[2,256,256]{2,1,0:T(8,128)}, f32[256,256]{1,0:T(8,128)}) async-done(((f32[2,256,256]{2,1,0:T(8,128)}, f32[256,256]{1,0:T(8,128)}), (f32[2,256,256]{2,1,0:T(8,128)}, f32[256,256]{1,0:T(8,128)})) %all-reduce.7.cloned.1.call-update) | async-done | bytes 786448 | tf_op jit(solution)/shard_map/psum | solution.py:130
  536.9 5.4 collective-permute-done.20
  543.3 10.0 %collective-permute-done.21 = f32[2,384,64]{2,1,0:T(8,128)S(1)} collective-permute-done((f32[2,384,64]{2,1,0:T(8,128)S(1)}, f32[2,384,64]{2,1,0:T(8,128)S(1)}, u32[]{:S(2)}, u32[]{:S(2)}) %collective-permute-start.21) | collective-permute-done | bytes 196640 | tf_op jit(solution)/shard_map/ppermute | solution.py:31
  564.1 4.6 collective-permute-start.24
  577.2 7.7 collective-permute-done.26
  584.9 10.9 %collective-permute-done.27 = f32[2,384,64]{2,1,0:T(8,128)S(1)} collective-permute-done((f32[2,384,64]{2,1,0:T(8,128)S(1)}, f32[2,384,64]{2,1,0:T(8,128)S(1)}, u32[]{:S(2)}, u32[]{:S(2)}) %collective-permute-start.27) | collective-permute-done | bytes 196640 | tf_op jit(solution)/shard_map/ppermute | solution.py:23
  630.7 4.2 collective-permute-start.28
  636.3 7.9 collective-permute-done.28
  645.3 10.4 %collective-permute-done.29 = f32[2,384,64]{2,1,0:T(8,128)S(1)} collective-permute-done((f32[2,384,64]{2,1,0:T(8,128)S(1)}, f32[2,384,64]{2,1,0:T(8,128)S(1)}, u32[]{:S(2)}, u32[]{:S(2)}) %collective-permute-start.29) | collective-permute-done | bytes 196640 | tf_op jit(solution)/shard_map/ppermute | solution.py:31
  666.7 247.8 %all-reduce.5.cloned.1.call-done = (f32[2,256,256]{2,1,0:T(8,128)}, f32[256,256]{1,0:T(8,128)}) async-done(((f32[2,256,256]{2,1,0:T(8,128)}, f32[256,256]{1,0:T(8,128)}), (f32[2,256,256]{2,1,0:T(8,128)}, f32[256,256]{1,0:T(8,128)})) %all-reduce.5.cloned.1.call-update) | async-done | bytes 786448 | tf_op jit(solution)/shard_map/psum | solution.py:130
  (264 shorter events, 236.0 us)
Async XLA Ops:
  7.2 480.8 %all-reduce.7.cloned.1.call-start = ((), (), s32[]{:S(2)}) async-start(), calls=%async_computation.1 | async-start | bytes 1572864 | tf_op jit(solution)/shard_map/psum | solution.py:130
  8.2 12.9 %collective-permute-start = (f32[2,64,128]{2,0,1:T(2,128)S(1)}, f32[2,64,128]{2,0,1:T(2,128)S(1)}, u32[]{:S(2)}, u32[]{:S(2)}) collective-permute-start(f32[2,64,128]{2,0,1:T(2,128)S(1)} %copy.230), channel_id=1, source_target_pairs={{0,8},{8,16},{16,24},{24,32},{32,40},{40,48},{48,56},{56,64},{64,7... | collective-permute-start | bytes 196616 | tf_op jit(solution)/shard_map/ppermute | solution.py:22
  10.2 11.2 %collective-permute-start.1 = (f32[2,64,128]{2,0,1:T(2,128)S(1)}, f32[2,64,128]{2,0,1:T(2,128)S(1)}, u32[]{:S(2)}, u32[]{:S(2)}) collective-permute-start(f32[2,64,128]{2,0,1:T(2,128)S(1)} %copy.231), channel_id=1, source_target_pairs={{8,0},{16,8},{24,16},{32,24},{40,32},{48,40},{56,48},{64,56},{72,6... | collective-permute-start | bytes 196616 | tf_op jit(solution)/shard_map/ppermute | solution.py:23
  21.8 13.1 %collective-permute-start.2 = (f32[2,384,64]{2,0,1:T(2,128)S(1)}, f32[2,384,64]{2,0,1:T(2,128)S(1)}, u32[]{:S(2)}, u32[]{:S(2)}) collective-permute-start(f32[2,384,64]{2,0,1:T(2,128)S(1)} %get-tuple-element.266), channel_id=1, source_target_pairs={{0,1},{1,2},{2,3},{3,4},{4,5},{5,6},{6,7},{8,9},{9,10},{10,11},{11... | collective-permute-start | bytes 589832 | tf_op jit(solution)/shard_map/ppermute | solution.py:22
  25.9 20.1 %collective-permute-start.3 = (f32[2,384,64]{2,0,1:T(2,128)S(1)}, f32[2,384,64]{2,0,1:T(2,128)S(1)}, u32[]{:S(2)}, u32[]{:S(2)}) collective-permute-start(f32[2,384,64]{2,0,1:T(2,128)S(1)} %get-tuple-element.267), channel_id=1, source_target_pairs={{1,0},{2,1},{3,2},{4,3},{5,4},{6,5},{7,6},{9,8},{10,9},{11,10},{12... | collective-permute-start | bytes 589832 | tf_op jit(solution)/shard_map/ppermute | solution.py:23
  90.8 13.2 %collective-permute-start.4 = (f32[2,384,64]{2,1,0:T(8,128)S(1)}, f32[2,384,64]{2,1,0:T(8,128)S(1)}, u32[]{:S(2)}, u32[]{:S(2)}) collective-permute-start(f32[2,384,64]{2,1,0:T(8,128)S(1)} %get-tuple-element.247), channel_id=1, source_target_pairs={{0,1},{1,2},{2,3},{3,4},{4,5},{5,6},{6,7},{8,9},{9,10},{10,11},{11... | collective-permute-start | bytes 589832 | tf_op jit(solution)/shard_map/ppermute | solution.py:31
  95.4 18.7 %collective-permute-start.5 = (f32[2,384,64]{2,1,0:T(8,128)S(1)}, f32[2,384,64]{2,1,0:T(8,128)S(1)}, u32[]{:S(2)}, u32[]{:S(2)}) collective-permute-start(f32[2,384,64]{2,1,0:T(8,128)S(1)} %get-tuple-element.246), channel_id=1, source_target_pairs={{1,0},{2,1},{3,2},{4,3},{5,4},{6,5},{7,6},{9,8},{10,9},{11,10},{12... | collective-permute-start | bytes 589832 | tf_op jit(solution)/shard_map/ppermute | solution.py:31
  115.9 7.0 collective-permute-start.6
  132.5 14.3 %collective-permute-start.10 = (f32[2,384,64]{2,1,0:T(8,128)S(1)}, f32[2,384,64]{2,1,0:T(8,128)S(1)}, u32[]{:S(2)}, u32[]{:S(2)}) collective-permute-start(f32[2,384,64]{2,1,0:T(8,128)S(1)} %get-tuple-element.262), channel_id=1, source_target_pairs={{0,1},{1,2},{2,3},{3,4},{4,5},{5,6},{6,7},{8,9},{9,10},{10,11},{11... | collective-permute-start | bytes 589832 | tf_op jit(solution)/shard_map/ppermute | solution.py:22
  137.7 18.8 %collective-permute-start.11 = (f32[2,384,64]{2,1,0:T(8,128)S(1)}, f32[2,384,64]{2,1,0:T(8,128)S(1)}, u32[]{:S(2)}, u32[]{:S(2)}) collective-permute-start(f32[2,384,64]{2,1,0:T(8,128)S(1)} %get-tuple-element.263), channel_id=1, source_target_pairs={{1,0},{2,1},{3,2},{4,3},{5,4},{6,5},{7,6},{9,8},{10,9},{11,10},{12... | collective-permute-start | bytes 589832 | tf_op jit(solution)/shard_map/ppermute | solution.py:23
  191.4 14.8 %collective-permute-start.12 = (f32[2,384,64]{2,1,0:T(8,128)S(1)}, f32[2,384,64]{2,1,0:T(8,128)S(1)}, u32[]{:S(2)}, u32[]{:S(2)}) collective-permute-start(f32[2,384,64]{2,1,0:T(8,128)S(1)} %get-tuple-element.245), channel_id=1, source_target_pairs={{0,1},{1,2},{2,3},{3,4},{4,5},{5,6},{6,7},{8,9},{9,10},{10,11},{11... | collective-permute-start | bytes 589832 | tf_op jit(solution)/shard_map/ppermute | solution.py:31
  196.9 18.5 %collective-permute-start.13 = (f32[2,384,64]{2,1,0:T(8,128)S(1)}, f32[2,384,64]{2,1,0:T(8,128)S(1)}, u32[]{:S(2)}, u32[]{:S(2)}) collective-permute-start(f32[2,384,64]{2,1,0:T(8,128)S(1)} %get-tuple-element.244), channel_id=1, source_target_pairs={{1,0},{2,1},{3,2},{4,3},{5,4},{6,5},{7,6},{9,8},{10,9},{11,10},{12... | collective-permute-start | bytes 589832 | tf_op jit(solution)/shard_map/ppermute | solution.py:31
  224.7 7.8 collective-permute-start.16
  232.5 682.0 %all-reduce.5.cloned.1.call-start = ((), (), s32[]{:S(2)}) async-start(), calls=%async_computation | async-start | bytes 1572864 | tf_op jit(solution)/shard_map/psum | solution.py:130
  233.7 256.4 %collective-permute-start.18 = (f32[2,384,64]{2,1,0:T(8,128)S(1)}, f32[2,384,64]{2,1,0:T(8,128)S(1)}, u32[]{:S(2)}, u32[]{:S(2)}) collective-permute-start(f32[2,384,64]{2,1,0:T(8,128)S(1)} %get-tuple-element.258), channel_id=1, source_target_pairs={{0,1},{1,2},{2,3},{3,4},{4,5},{5,6},{6,7},{8,9},{9,10},{10,11},{11... | collective-permute-start | bytes 589832 | tf_op jit(solution)/shard_map/ppermute | solution.py:22
  235.1 255.1 %collective-permute-start.19 = (f32[2,384,64]{2,1,0:T(8,128)S(1)}, f32[2,384,64]{2,1,0:T(8,128)}, u32[]{:S(2)}, u32[]{:S(2)}) collective-permute-start(f32[2,384,64]{2,1,0:T(8,128)S(1)} %get-tuple-element.259), channel_id=1, source_target_pairs={{1,0},{2,1},{3,2},{4,3},{5,4},{6,5},{7,6},{9,8},{10,9},{11,10},{12... | collective-permute-start | bytes 589832 | tf_op jit(solution)/shard_map/ppermute | solution.py:23
  531.4 10.8 %collective-permute-start.20 = (f32[2,384,64]{2,1,0:T(8,128)S(1)}, f32[2,384,64]{2,1,0:T(8,128)S(1)}, u32[]{:S(2)}, u32[]{:S(2)}) collective-permute-start(f32[2,384,64]{2,1,0:T(8,128)S(1)} %get-tuple-element.243), channel_id=1, source_target_pairs={{0,1},{1,2},{2,3},{3,4},{4,5},{5,6},{6,7},{8,9},{9,10},{10,11},{11... | collective-permute-start | bytes 589832 | tf_op jit(solution)/shard_map/ppermute | solution.py:31
  535.6 17.8 %collective-permute-start.21 = (f32[2,384,64]{2,1,0:T(8,128)S(1)}, f32[2,384,64]{2,1,0:T(8,128)S(1)}, u32[]{:S(2)}, u32[]{:S(2)}) collective-permute-start(f32[2,384,64]{2,1,0:T(8,128)S(1)} %get-tuple-element.242), channel_id=1, source_target_pairs={{1,0},{2,1},{3,2},{4,3},{5,4},{6,5},{7,6},{9,8},{10,9},{11,10},{12... | collective-permute-start | bytes 589832 | tf_op jit(solution)/shard_map/ppermute | solution.py:31
  555.1 7.0 collective-permute-start.22
  572.7 12.3 %collective-permute-start.26 = (f32[2,384,64]{2,1,0:T(8,128)S(1)}, f32[2,384,64]{2,1,0:T(8,128)S(1)}, u32[]{:S(2)}, u32[]{:S(2)}) collective-permute-start(f32[2,384,64]{2,1,0:T(8,128)S(1)} %get-tuple-element.254), channel_id=1, source_target_pairs={{0,1},{1,2},{2,3},{3,4},{4,5},{5,6},{6,7},{8,9},{9,10},{10,11},{11... | collective-permute-start | bytes 589832 | tf_op jit(solution)/shard_map/ppermute | solution.py:22
  575.9 19.9 %collective-permute-start.27 = (f32[2,384,64]{2,1,0:T(8,128)S(1)}, f32[2,384,64]{2,1,0:T(8,128)S(1)}, u32[]{:S(2)}, u32[]{:S(2)}) collective-permute-start(f32[2,384,64]{2,1,0:T(8,128)S(1)} %get-tuple-element.255), channel_id=1, source_target_pairs={{1,0},{2,1},{3,2},{4,3},{5,4},{6,5},{7,6},{9,8},{10,9},{11,10},{12... | collective-permute-start | bytes 589832 | tf_op jit(solution)/shard_map/ppermute | solution.py:23
  630.7 13.5 %collective-permute-start.28 = (f32[2,384,64]{2,1,0:T(8,128)S(1)}, f32[2,384,64]{2,1,0:T(8,128)S(1)}, u32[]{:S(2)}, u32[]{:S(2)}) collective-permute-start(f32[2,384,64]{2,1,0:T(8,128)S(1)} %get-tuple-element.241), channel_id=1, source_target_pairs={{0,1},{1,2},{2,3},{3,4},{4,5},{5,6},{6,7},{8,9},{9,10},{10,11},{11... | collective-permute-start | bytes 589832 | tf_op jit(solution)/shard_map/ppermute | solution.py:31
  635.0 20.6 %collective-permute-start.29 = (f32[2,384,64]{2,1,0:T(8,128)S(1)}, f32[2,384,64]{2,1,0:T(8,128)S(1)}, u32[]{:S(2)}, u32[]{:S(2)}) collective-permute-start(f32[2,384,64]{2,1,0:T(8,128)S(1)} %get-tuple-element.240), channel_id=1, source_target_pairs={{1,0},{2,1},{3,2},{4,3},{5,4},{6,5},{7,6},{9,8},{10,9},{11,10},{12... | collective-permute-start | bytes 589832 | tf_op jit(solution)/shard_map/ppermute | solution.py:31
  657.4 6.6 collective-permute-start.30
  (27 other events, 764.4 us)
Sparse Core Ops, SparseCore 0:
  232.6 255.3 all-reduce.6
  660.5 253.9 all-reduce.4
where the time goes:
time: 935 us; the launch traced here: 925 us
  waiting for transfers between devices  632 us (68%)
  matrix products  95.6 us (10%)
  starting transfers between devices  89.1 us (10%)
  local copies, waits for them, and re-layouts  66.5 us (7%)
  between operations  23.1 us (2%)
  other arithmetic  18 us (2%)
    psum x2, waiting for transfers between devices, per_device(): lax.psum((grad_sum, light_sum), ('stripe', 'tile'))  499 us
    ppermute x16, waiting for transfers between devices, from_behind(): lax.ppermute(value, axis, [(source, source + steps) for source in range(f...  73.4 us
    dot_general x32, matrix products, apply_right(): jnp.einsum('pkn,nm->pkm', batch, matrix, preferred_element_type=jnp.float32)  56.7 us
    ppermute x16, starting transfers between devices, from_behind(): lax.ppermute(value, axis, [(source, source + steps) for source in range(f...  45.5 us
    dot_general x32, matrix products, apply_left(): jnp.einsum('kn,pnm->pkm', matrix, batch, preferred_element_type=jnp.float32)  38.9 us
    ppermute x8, waiting for transfers between devices, padded(): after = lax.ppermute(first, axis, down)  36.3 us
    dynamic_update_slice x12, local copies, waits for them, and re-layouts, per_device(): lax.dynamic_update_slice(gradient, before + object_grad[pattern], where)  33.7 us
    ppermute x8, starting transfers between devices, padded(): before = lax.ppermute(last, axis, up)  28.4 us
  transfers between devices with their start and end apart: 34, of which 23 were waited for; matrix products, arithmetic and copies ran while one was open for 1% of the time, Pallas kernels for 0%

commit v1 on v0

--- a/solution.py
+++ b/solution.py
@@ -127,7 +127,7 @@
             own_grad = own_grad.at[:, :HALO, :].add(from_above)
             own_grad = own_grad.at[:, PW - HALO :, :].add(from_below)
             current = current - step_size * own_grad
-        total_grad, total_light = lax.psum((grad_sum, light_sum), ("stripe", "tile"))
+        total_grad, total_light = lax.psum(lax.psum((grad_sum, light_sum), "tile"), "stripe")
         probe_field = probe_field - 0.5 * total_grad / (total_light + 1.0)
     return (current, probe_field)
 

time: 935 us -> 1030 us (1.10)
  waiting for transfers between devices: 632 us -> 716 us
    psum x2 -> x4, waiting for transfers between devices: 499 us -> 558 us  [the longest x2 421 us: per_device(): lax.psum(lax.psum((grad_sum, light_sum), 'tile'), 'stripe')]
    ppermute x8, waiting for transfers between devices: 36.3 us -> 48.1 us  [padded(): after = lax.ppermute(first, axis, down)]
  transfers between devices with their start and end apart: 34 -> 36, of which waited for: 23 -> 27; matrix products, arithmetic and copies ran while one was open for 1% -> 2% of each run, Pallas kernels for 0% -> 0%
where the time goes in v1:
time: 1030 us; the launch traced here: 1010 us
  waiting for transfers between devices  716 us (70%)
  matrix products  95.6 us (9%)
  starting transfers between devices  90.3 us (9%)
  local copies, waits for them, and re-layouts  67.9 us (7%)
  between operations  23.1 us (2%)
  other arithmetic  18.1 us (2%)
    psum x2, waiting for transfers between devices, per_device(): lax.psum(lax.psum((grad_sum, light_sum), 'tile'), 'stripe')  421 us
    psum x2, waiting for transfers between devices, per_device(): lax.psum((grad_sum, light_sum), 'tile')  137 us
    ppermute x16, waiting for transfers between devices, from_behind(): lax.ppermute(value, axis, [(source, source + steps) for source in range(f...  82.9 us
    dot_general x32, matrix products, apply_right(): jnp.einsum('pkn,nm->pkm', batch, matrix, preferred_element_type=jnp.float32)  56.8 us
    ppermute x8, waiting for transfers between devices, padded(): after = lax.ppermute(first, axis, down)  48.1 us
    ppermute x16, starting transfers between devices, from_behind(): lax.ppermute(value, axis, [(source, source + steps) for source in range(f...  46.1 us
    dot_general x32, matrix products, apply_left(): jnp.einsum('kn,pnm->pkm', matrix, batch, preferred_element_type=jnp.float32)  38.9 us
    dynamic_update_slice x12, local copies, waits for them, and re-layouts, per_device(): lax.dynamic_update_slice(gradient, before + object_grad[pattern], where)  33.7 us
  transfers between devices with their start and end apart: 36, of which 27 were waited for; matrix products, arithmetic and copies ran while one was open for 2% of the time, Pallas kernels for 0%

profile of v1, /device:TPU:2, one launch (start us, length us, event | category | flops | bytes accessed | tf_op | source)
XLA Modules:
  0.0 1011.4 jit_solution(14178130225365209806)
XLA Ops:
  27.7 7.7 collective-permute-done.2
  35.4 11.0 %collective-permute-done.3 = f32[2,384,64]{2,0,1:T(2,128)S(1)} collective-permute-done((f32[2,384,64]{2,0,1:T(2,128)S(1)}, f32[2,384,64]{2,0,1:T(2,128)S(1)}, u32[]{:S(2)}, u32[]{:S(2)}) %collective-permute-start.3) | collective-permute-done | bytes 196640 | tf_op jit(solution)/shard_map/ppermute | solution.py:23
  70.8 12.6 %subtract_bitcast_fusion.3 = (f32[3,1,256,256]{3,2,0,1:T(8,128)S(1)}, f32[3,1,256,256]{3,2,0,1:T(8,128)S(1)}) fusion(f32[3,256,256]{2,1,0:T(8,128)S(1)} %convolution_add_fusion.12, f32[256,256]{1,0:T(8,128)S(1)} %get-tuple-element.255, f32[256,256]{1,0:T(8,128)S(1)} %get-tuple-element.254, f32[3,256,256]{2,1,0:T(8,128)S(1)} %fusion.160, ...), kind=kOutput, calls=%fused_computation.134 | convolution fusion | flops 103088128 | bytes 4063232 | tf_op jit(solution)/shard_map/pkn,nm->pkm/dot_general | solution.py:50
  97.2 7.2 collective-permute-done.4
  105.5 9.0 collective-permute-done.5
  133.0 5.2 collective-permute-start.10
  139.4 7.8 collective-permute-done.10
  147.3 9.7 collective-permute-done.11
  191.8 5.3 collective-permute-start.12
  198.6 8.0 collective-permute-done.12
  207.7 8.1 collective-permute-done.13
  226.1 5.0 collective-permute-start.16
  234.9 77.4 %all-reduce.15.cloned.1.call-done = (f32[2,256,256]{2,1,0:T(8,128)}, f32[256,256]{1,0:T(8,128)}) async-done(((f32[2,256,256]{2,1,0:T(8,128)}, f32[256,256]{1,0:T(8,128)}), (f32[2,256,256]{2,1,0:T(8,128)}, f32[256,256]{1,0:T(8,128)})) %all-reduce.15.cloned.1.call-update) | async-done | bytes 786448 | tf_op jit(solution)/shard_map/psum | solution.py:130
  319.9 10.4 %collective-permute-done.19 = f32[2,384,64]{2,1,0:T(8,128)S(1)} collective-permute-done((f32[2,384,64]{2,1,0:T(8,128)S(1)}, f32[2,384,64]{2,1,0:T(8,128)S(1)}, u32[]{:S(2)}, u32[]{:S(2)}) %collective-permute-start.19) | collective-permute-done | bytes 196640 | tf_op jit(solution)/shard_map/ppermute | solution.py:23
  336.3 202.7 %all-reduce.11.cloned.1.call-done = (f32[2,256,256]{2,1,0:T(8,128)}, f32[256,256]{1,0:T(8,128)}) async-done(((f32[2,256,256]{2,1,0:T(8,128)}, f32[256,256]{1,0:T(8,128)}), (f32[2,256,256]{2,1,0:T(8,128)}, f32[256,256]{1,0:T(8,128)})) %all-reduce.11.cloned.1.call-update) | async-done | bytes 786448 | tf_op jit(solution)/shard_map/psum | solution.py:130
  582.3 7.3 collective-permute-done.20
  590.8 10.0 collective-permute-done.21
  605.8 4.6 collective-permute-start.23
  625.3 7.8 collective-permute-done.26
  633.1 11.4 %collective-permute-done.27 = f32[2,384,64]{2,1,0:T(8,128)S(1)} collective-permute-done((f32[2,384,64]{2,1,0:T(8,128)S(1)}, f32[2,384,64]{2,1,0:T(8,128)S(1)}, u32[]{:S(2)}, u32[]{:S(2)}) %collective-permute-start.27) | collective-permute-done | bytes 196640 | tf_op jit(solution)/shard_map/ppermute | solution.py:23
  686.7 9.3 collective-permute-done.28
  697.1 16.6 %collective-permute-done.29 = f32[2,384,64]{2,1,0:T(8,128)S(1)} collective-permute-done((f32[2,384,64]{2,1,0:T(8,128)S(1)}, f32[2,384,64]{2,1,0:T(8,128)S(1)}, u32[]{:S(2)}, u32[]{:S(2)}) %collective-permute-start.29) | collective-permute-done | bytes 196640 | tf_op jit(solution)/shard_map/ppermute | solution.py:31
  715.4 59.7 %all-reduce.13.cloned.1.call-done = (f32[2,256,256]{2,1,0:T(8,128)}, f32[256,256]{1,0:T(8,128)}) async-done(((f32[2,256,256]{2,1,0:T(8,128)}, f32[256,256]{1,0:T(8,128)}), (f32[2,256,256]{2,1,0:T(8,128)}, f32[256,256]{1,0:T(8,128)})) %all-reduce.13.cloned.1.call-update) | async-done | bytes 786448 | tf_op jit(solution)/shard_map/psum | solution.py:130
  783.4 218.1 %all-reduce.9.cloned.1.call-done = (f32[2,256,256]{2,1,0:T(8,128)}, f32[256,256]{1,0:T(8,128)}) async-done(((f32[2,256,256]{2,1,0:T(8,128)}, f32[256,256]{1,0:T(8,128)}), (f32[2,256,256]{2,1,0:T(8,128)}, f32[256,256]{1,0:T(8,128)})) %all-reduce.9.cloned.1.call-update) | async-done | bytes 786448 | tf_op jit(solution)/shard_map/psum | solution.py:130
  (270 shorter events, 256.4 us)
Async XLA Ops:
  7.2 305.2 %all-reduce.15.cloned.1.call-start = ((), (), s32[]{:S(2)}) async-start(), calls=%async_computation.3 | async-start | bytes 1572864 | tf_op jit(solution)/shard_map/psum | solution.py:130
  8.2 13.3 %collective-permute-start = (f32[2,64,128]{2,0,1:T(2,128)S(1)}, f32[2,64,128]{2,0,1:T(2,128)S(1)}, u32[]{:S(2)}, u32[]{:S(2)}) collective-permute-start(f32[2,64,128]{2,0,1:T(2,128)S(1)} %copy.230), channel_id=1, source_target_pairs={{0,8},{8,16},{16,24},{24,32},{32,40},{40,48},{48,56},{56,64},{64,7... | collective-permute-start | bytes 196616 | tf_op jit(solution)/shard_map/ppermute | solution.py:22
  10.2 11.6 %collective-permute-start.1 = (f32[2,64,128]{2,0,1:T(2,128)S(1)}, f32[2,64,128]{2,0,1:T(2,128)S(1)}, u32[]{:S(2)}, u32[]{:S(2)}) collective-permute-start(f32[2,64,128]{2,0,1:T(2,128)S(1)} %copy.231), channel_id=1, source_target_pairs={{8,0},{16,8},{24,16},{32,24},{40,32},{48,40},{56,48},{64,56},{72,6... | collective-permute-start | bytes 196616 | tf_op jit(solution)/shard_map/ppermute | solution.py:23
  22.3 13.1 %collective-permute-start.2 = (f32[2,384,64]{2,0,1:T(2,128)S(1)}, f32[2,384,64]{2,0,1:T(2,128)S(1)}, u32[]{:S(2)}, u32[]{:S(2)}) collective-permute-start(f32[2,384,64]{2,0,1:T(2,128)S(1)} %get-tuple-element.270), channel_id=1, source_target_pairs={{0,1},{1,2},{2,3},{3,4},{4,5},{5,6},{6,7},{8,9},{9,10},{10,11},{11... | collective-permute-start | bytes 589832 | tf_op jit(solution)/shard_map/ppermute | solution.py:22
  26.3 20.1 %collective-permute-start.3 = (f32[2,384,64]{2,0,1:T(2,128)S(1)}, f32[2,384,64]{2,0,1:T(2,128)S(1)}, u32[]{:S(2)}, u32[]{:S(2)}) collective-permute-start(f32[2,384,64]{2,0,1:T(2,128)S(1)} %get-tuple-element.271), channel_id=1, source_target_pairs={{1,0},{2,1},{3,2},{4,3},{5,4},{6,5},{7,6},{9,8},{10,9},{11,10},{12... | collective-permute-start | bytes 589832 | tf_op jit(solution)/shard_map/ppermute | solution.py:23
  91.2 13.2 %collective-permute-start.4 = (f32[2,384,64]{2,1,0:T(8,128)S(1)}, f32[2,384,64]{2,1,0:T(8,128)S(1)}, u32[]{:S(2)}, u32[]{:S(2)}) collective-permute-start(f32[2,384,64]{2,1,0:T(8,128)S(1)} %get-tuple-element.251), channel_id=1, source_target_pairs={{0,1},{1,2},{2,3},{3,4},{4,5},{5,6},{6,7},{8,9},{9,10},{10,11},{11... | collective-permute-start | bytes 589832 | tf_op jit(solution)/shard_map/ppermute | solution.py:31
  95.9 18.7 %collective-permute-start.5 = (f32[2,384,64]{2,1,0:T(8,128)S(1)}, f32[2,384,64]{2,1,0:T(8,128)S(1)}, u32[]{:S(2)}, u32[]{:S(2)}) collective-permute-start(f32[2,384,64]{2,1,0:T(8,128)S(1)} %get-tuple-element.250), channel_id=1, source_target_pairs={{1,0},{2,1},{3,2},{4,3},{5,4},{6,5},{7,6},{9,8},{10,9},{11,10},{12... | collective-permute-start | bytes 589832 | tf_op jit(solution)/shard_map/ppermute | solution.py:31
  116.3 7.0 collective-permute-start.6
  133.0 14.3 %collective-permute-start.10 = (f32[2,384,64]{2,1,0:T(8,128)S(1)}, f32[2,384,64]{2,1,0:T(8,128)S(1)}, u32[]{:S(2)}, u32[]{:S(2)}) collective-permute-start(f32[2,384,64]{2,1,0:T(8,128)S(1)} %get-tuple-element.266), channel_id=1, source_target_pairs={{0,1},{1,2},{2,3},{3,4},{4,5},{5,6},{6,7},{8,9},{9,10},{10,11},{11... | collective-permute-start | bytes 589832 | tf_op jit(solution)/shard_map/ppermute | solution.py:22
  138.1 18.8 %collective-permute-start.11 = (f32[2,384,64]{2,1,0:T(8,128)S(1)}, f32[2,384,64]{2,1,0:T(8,128)S(1)}, u32[]{:S(2)}, u32[]{:S(2)}) collective-permute-start(f32[2,384,64]{2,1,0:T(8,128)S(1)} %get-tuple-element.267), channel_id=1, source_target_pairs={{1,0},{2,1},{3,2},{4,3},{5,4},{6,5},{7,6},{9,8},{10,9},{11,10},{12... | collective-permute-start | bytes 589832 | tf_op jit(solution)/shard_map/ppermute | solution.py:23
  191.8 14.8 %collective-permute-start.12 = (f32[2,384,64]{2,1,0:T(8,128)S(1)}, f32[2,384,64]{2,1,0:T(8,128)S(1)}, u32[]{:S(2)}, u32[]{:S(2)}) collective-permute-start(f32[2,384,64]{2,1,0:T(8,128)S(1)} %get-tuple-element.249), channel_id=1, source_target_pairs={{0,1},{1,2},{2,3},{3,4},{4,5},{5,6},{6,7},{8,9},{9,10},{10,11},{11... | collective-permute-start | bytes 589832 | tf_op jit(solution)/shard_map/ppermute | solution.py:31
  197.3 18.5 %collective-permute-start.13 = (f32[2,384,64]{2,1,0:T(8,128)S(1)}, f32[2,384,64]{2,1,0:T(8,128)S(1)}, u32[]{:S(2)}, u32[]{:S(2)}) collective-permute-start(f32[2,384,64]{2,1,0:T(8,128)S(1)} %get-tuple-element.248), channel_id=1, source_target_pairs={{1,0},{2,1},{3,2},{4,3},{5,4},{6,5},{7,6},{9,8},{10,9},{11,10},{12... | collective-permute-start | bytes 589832 | tf_op jit(solution)/shard_map/ppermute | solution.py:31
  220.4 318.6 %all-reduce.11.cloned.1.call-start = ((), (), s32[]{:S(2)}) async-start(), calls=%async_computation.1 | async-start | bytes 1572864 | tf_op jit(solution)/shard_map/psum | solution.py:130
  312.4 462.7 %all-reduce.13.cloned.1.call-start = ((), (), s32[]{:S(2)}) async-start(), calls=%async_computation.2 | async-start | bytes 1572864 | tf_op jit(solution)/shard_map/psum | solution.py:130
  312.6 7.3 collective-permute-start.18
  314.6 15.7 %collective-permute-start.19 = (f32[2,384,64]{2,1,0:T(8,128)S(1)}, f32[2,384,64]{2,1,0:T(8,128)S(1)}, u32[]{:S(2)}, u32[]{:S(2)}) collective-permute-start(f32[2,384,64]{2,1,0:T(8,128)S(1)} %get-tuple-element.263), channel_id=1, source_target_pairs={{1,0},{2,1},{3,2},{4,3},{5,4},{6,5},{7,6},{9,8},{10,9},{11,10},{12... | collective-permute-start | bytes 589832 | tf_op jit(solution)/shard_map/ppermute | solution.py:23
  576.8 12.8 %collective-permute-start.20 = (f32[2,384,64]{2,1,0:T(8,128)S(1)}, f32[2,384,64]{2,1,0:T(8,128)S(1)}, u32[]{:S(2)}, u32[]{:S(2)}) collective-permute-start(f32[2,384,64]{2,1,0:T(8,128)S(1)} %get-tuple-element.247), channel_id=1, source_target_pairs={{0,1},{1,2},{2,3},{3,4},{4,5},{5,6},{6,7},{8,9},{9,10},{10,11},{11... | collective-permute-start | bytes 589832 | tf_op jit(solution)/shard_map/ppermute | solution.py:31
  581.0 19.7 %collective-permute-start.21 = (f32[2,384,64]{2,1,0:T(8,128)S(1)}, f32[2,384,64]{2,1,0:T(8,128)S(1)}, u32[]{:S(2)}, u32[]{:S(2)}) collective-permute-start(f32[2,384,64]{2,1,0:T(8,128)S(1)} %get-tuple-element.246), channel_id=1, source_target_pairs={{1,0},{2,1},{3,2},{4,3},{5,4},{6,5},{7,6},{9,8},{10,9},{11,10},{12... | collective-permute-start | bytes 589832 | tf_op jit(solution)/shard_map/ppermute | solution.py:31
  602.5 7.9 collective-permute-start.22
  620.1 12.9 %collective-permute-start.26 = (f32[2,384,64]{2,1,0:T(8,128)S(1)}, f32[2,384,64]{2,1,0:T(8,128)S(1)}, u32[]{:S(2)}, u32[]{:S(2)}) collective-permute-start(f32[2,384,64]{2,1,0:T(8,128)S(1)} %get-tuple-element.258), channel_id=1, source_target_pairs={{0,1},{1,2},{2,3},{3,4},{4,5},{5,6},{6,7},{8,9},{9,10},{10,11},{11... | collective-permute-start | bytes 589832 | tf_op jit(solution)/shard_map/ppermute | solution.py:22
  624.0 20.4 %collective-permute-start.27 = (f32[2,384,64]{2,1,0:T(8,128)S(1)}, f32[2,384,64]{2,1,0:T(8,128)S(1)}, u32[]{:S(2)}, u32[]{:S(2)}) collective-permute-start(f32[2,384,64]{2,1,0:T(8,128)S(1)} %get-tuple-element.259), channel_id=1, source_target_pairs={{1,0},{2,1},{3,2},{4,3},{5,4},{6,5},{7,6},{9,8},{10,9},{11,10},{12... | collective-permute-start | bytes 589832 | tf_op jit(solution)/shard_map/ppermute | solution.py:23
  681.0 320.5 %all-reduce.9.cloned.1.call-start = ((), (), s32[]{:S(2)}) async-start(), calls=%async_computation | async-start | bytes 1572864 | tf_op jit(solution)/shard_map/psum | solution.py:130
  681.2 14.7 %collective-permute-start.28 = (f32[2,384,64]{2,1,0:T(8,128)S(1)}, f32[2,384,64]{2,1,0:T(8,128)S(1)}, u32[]{:S(2)}, u32[]{:S(2)}) collective-permute-start(f32[2,384,64]{2,1,0:T(8,128)S(1)} %get-tuple-element.245), channel_id=1, source_target_pairs={{0,1},{1,2},{2,3},{3,4},{4,5},{5,6},{6,7},{8,9},{9,10},{10,11},{11... | collective-permute-start | bytes 589832 | tf_op jit(solution)/shard_map/ppermute | solution.py:31
  685.4 28.2 %collective-permute-start.29 = (f32[2,384,64]{2,1,0:T(8,128)S(1)}, f32[2,384,64]{2,1,0:T(8,128)S(1)}, u32[]{:S(2)}, u32[]{:S(2)}) collective-permute-start(f32[2,384,64]{2,1,0:T(8,128)S(1)} %get-tuple-element.244), channel_id=1, source_target_pairs={{1,0},{2,1},{3,2},{4,3},{5,4},{6,5},{7,6},{9,8},{10,9},{11,10},{12... | collective-permute-start | bytes 589832 | tf_op jit(solution)/shard_map/ppermute | solution.py:31
  (29 other events, 599.6 us)
Sparse Core Ops, SparseCore 0:
  220.5 91.8 all-reduce.14
  315.0 223.9 all-reduce.10
  681.1 93.9 all-reduce.12
  777.6 223.8 all-reduce.8
